TPU v7x, 32 devices: a whole 2x2x4 slice. The times are simulated.
32 devices in a mesh: lon: 8 (over z, y), lat: 4 (over x, core).
Axes of the slice: x: 2, y: 2, z: 4, core: 2. Of those that a mesh axis runs over, the one named last changes fastest.
Arguments:
- perturbation: float32 [80, 128, 4096], P(None, 'lon', 'lat'), may hold values from -6 to 6
- weight_table: float32 [8, 2048], P(None, 'lat'), may hold values from 0.1 to 1
- band_index: int32 [13], replicated, may hold values from 0 to 7
Outputs:
- localized: float32 [80, 128, 4096], P(None, 'lon', 'lat')
Inputs may be any that keep to these rules, and one draw needn't show every extreme that they name: `band_index`: each entry names a row of weight_table.
All inputs are finite; a program needn't handle non-finite values.
Results may differ from a plain program's by a relative error of at most 0.00005.
Values sent between devices are 32-bit elements; how exact they have to be, the bound alone decides.
No kernel may reach another device: no remote copies, remote signals or barrier semaphores. Data moves between devices by JAX's collectives and lax.ppermute only.
A program may use at most 128 MiB of HBM per device.

v0:
```python
import math

import jax
import jax.numpy as jnp
from jax import lax
from jax.experimental import pallas as pl
from jax.experimental.pallas import tpu as pltpu
from jax.sharding import PartitionSpec as P


LEVELS = 4
LANES = 128
SUB = 8
BLOCK = 40
SEND_STACK = 4
INNER_STACK = 2
OUTER_STACK = 6
HALO = 32

root_three = math.sqrt(3.0)
tap_1 = (3.0 + root_three) / (4.0 * math.sqrt(2.0))
tap_2 = (3.0 - root_three) / (4.0 * math.sqrt(2.0))
tap_3 = (1.0 - root_three) / (4.0 * math.sqrt(2.0))
T = tap_3 / tap_2
Q = tap_2 / tap_1


RIGHT = {"c1": 0, "a1": 4, "a2": 8, "k": 10, "edge": 11}
LEFT = {"b1": 0, "b2": 4, "b3": 6, "edge": 7}
RIGHT_SIZE = 13
LEFT_SIZE = 8
EDGE = {
    "c1": (0, 0, 2),
    "a1": (0, 1, 2),
    "a0": (0, 64, 1),
    "a2": (1, 0, 4),
    "k": (1, 1, 8),
    "b1": (0, 0, 2),
    "b2": (0, 1, 4),
    "b3": (0, 3, 8),
    "b0": (0, 64, 1),
}
COUNT = {"c1": 4, "a1": 4, "b1": 4, "a2": 2, "b2": 2, "k": 1, "b3": 1}
MAINS = (4, 2, 1, 1)
WEIGHTS = {}
WEIGHT_COUNT = 0
for level_at in range(LEVELS):
    for band_at in range(3 if level_at < LEVELS - 1 else 4):
        WEIGHTS[level_at, band_at] = WEIGHT_COUNT
        WEIGHT_COUNT += MAINS[level_at] + 1


def turn(v, by):
    by = by % LANES
    return v if by == 0 else pltpu.roll(v, by, 1)


def pick(v, index):
    return jnp.take_along_axis(v, index, axis=1, mode="promise_in_bounds")


class Lanes:
    def __init__(self, rows):
        l = lax.broadcasted_iota(jnp.int32, (rows, LANES), 1)
        self.l = l
        self.zero = jnp.zeros((rows, LANES), jnp.float32)
        self.bit = [(l & (1 << level)) == 0 for level in range(LEVELS)]
        self.ahead, self.behind = [], []
        for level in range(LEVELS):
            stride = 2 << level
            bits = min(level + 1, 3)
            ahead, behind = (l + stride) & (LANES - 1), (l - stride) & (LANES - 1)
            flip = lambda x: int(format(x, "0%db" % bits)[::-1], 2)
            for x in range(1 << bits):
                after = flip((flip(x) + 1) % (1 << bits))
                ahead = jnp.where(l == LANES - stride + x, after, ahead)
                behind = jnp.where(l == after, LANES - stride + x, behind)
            self.ahead.append(ahead)
            self.behind.append(behind)

    def split(self, row, level):
        main, edge = row[:-1], row[-1]
        d, stride, bit, l = 1 << level, 2 << level, self.bit[level], self.l
        half = len(main) // 2
        right = [turn(main[j + half], d) for j in range(half)]
        left = [turn(main[j], -d) for j in range(half)] or [turn(main[0], -d)]
        left.append(turn(edge, -d))
        if half:
            evens = [jnp.where(bit, main[j], right[j]) for j in range(half)]
            odds = [jnp.where(bit, left[j], main[j + half]) for j in range(half)]
        else:
            evens, odds = [main[0]], [left[0]]
        evens.append(edge)
        odds.append(left[-1])
        a = [o - T * e for e, o in zip(evens, odds)]
        b = [e + T * o for e, o in zip(evens, odds)]
        n = len(b) - 1
        first, beyond = b[0], b[-1]
        shifted = [turn(jnp.where(l < stride, b[j + 1], b[j]), -stride) for j in range(n - 1)]
        m = jnp.where(l == 0, beyond, first)
        shifted.append(pick(m if n == 1 else jnp.where(l < stride, m, b[n - 1]), self.ahead[level]))
        shifted.append(turn(jnp.where(l == 0, first, beyond), -stride))
        return a, shifted

    def analyze(self, row, level):
        a, b = self.split(row, level)
        return [i + Q * j for i, j in zip(a, b)], [j - Q * i for i, j in zip(a, b)]

    def low(self, row, level):
        a, b = self.split(row, level)
        return [i + Q * j for i, j in zip(a, b)]

    def join(self, a, b, level):
        d, stride, bit, l = 1 << level, 2 << level, self.bit[level], self.l
        n = len(b) - 1
        top = l >= LANES - stride
        before = turn(b[-1], stride)
        m = b[0] if n == 1 else jnp.where(top, b[n - 1], b[0])
        shifted = [pick(m, self.behind[level])]
        shifted += [turn(jnp.where(top, b[j - 1], b[j]), stride) for j in range(1, n)]
        shifted[0] = jnp.where(l == 0, before, shifted[0])
        if level > 0:
            shifted.append(before)
        evens = [s - T * i for i, s in zip(a, shifted)]
        odds = [i + T * s for i, s in zip(a, shifted)]
        right = [turn(o, d) for o in odds]
        left = [turn(e, -d) for e in evens[:n]] if level < LEVELS - 1 else []
        row = [jnp.where(bit, e, o) for e, o in zip(evens[:n], right)]
        row += [jnp.where(bit, e, o) for e, o in zip(left, odds)]
        if level > 0:
            row.append(jnp.where(bit, evens[n], right[n]))
        return row

    def synthesize(self, low, high, level):
        a = [i - Q * j for i, j in zip(low, high)]
        b = [j + Q * i for i, j in zip(low, high)]
        return self.join(a, b, level)

    def fill(self, edges, item, value):
        at, by, every = EDGE[item]
        l = (self.l - by) & (LANES - 1)
        here = (((l - 64 - HALO) & (LANES - 1)) < 64) & ((l & (every - 1)) == 0)
        edges[at] = jnp.where(here, turn(value, by), edges[at])


class Stacks:
    def __init__(self, block):
        self.block = block
        self.kinds = {}

    def of(self, count):
        if count not in self.kinds:
            self.kinds[count] = Lanes(count * self.block)
        return self.kinds[count]

    def stack(self, rows):
        return [jnp.concatenate(list(v), 0) if len(v) > 1 else v[0] for v in zip(*rows)]

    def unstack(self, row, count):
        return [[v[self.block * i : self.block * (i + 1)] for v in row] for i in range(count)]

    def analyze(self, rows, level):
        n = len(rows)
        low, high = self.of(n).analyze(self.stack(rows), level)
        return self.unstack(low, n), self.unstack(high, n)

    def low(self, rows, level):
        n = len(rows)
        return self.unstack(self.of(n).low(self.stack(rows), level), n)

    def join(self, a, b, level):
        n = len(a)
        return self.unstack(self.of(n).join(self.stack(a), self.stack(b), level), n)

    def synthesize(self, low, high, level):
        n = len(low)
        return self.unstack(self.of(n).synthesize(self.stack(low), self.stack(high), level), n)


def plus(x, y, scale=1.0):
    return [i + (j if scale == 1.0 else scale * j) for i, j in zip(x, y)]


def times(scale, x):
    return [scale * i for i in x]


def mul(x, y):
    return [i * j for i, j in zip(x, y)]


def pair(x0, x1):
    return plus(x1, x0, -T), plus(x0, x1, T)


def unpair(a, b):
    return plus(b, a, -T), plus(a, b, T)


def read_row(x_refs, left_ref, right_ref, lon, lons, k):
    rows = k.l.shape[0]
    row = [x_ref[pl.ds(lon, rows, stride=lons), :] for x_ref in x_refs]
    group, within = divmod(lon, lons // 4)
    beyond = turn(right_ref[within], -HALO * group)
    before = turn(left_ref[within], LANES - HALO - HALO * group)
    row.append(jnp.where(k.l < LANES // 2, beyond, before))
    return row


def put(ref, at, values):
    for i, v in enumerate(values):
        ref[:, pl.ds(LANES * (at + i), LANES)] = v


def get(ref, at, count):
    return [ref[:, pl.ds(LANES * (at + i), LANES)] for i in range(count)]


def first_kernel(lons, block, x_refs, table_ref, to_left_ref, to_right_ref, a_ref, b_ref):
    k = Lanes(block)
    groups = lons // 4

    def row(lon):
        return [x_ref[pl.ds(lon, block, stride=lons), :] for x_ref in x_refs]

    put(b_ref, 0, pair(row(0), row(1))[1])
    put(a_ref, 0, pair(row(lons - 2), row(lons - 1))[0])
    at = pl.ds(pl.multiple_of(pl.program_id(0) * block, block), block)
    for within in range(groups):
        to_left = to_right = None
        for group in range(4):
            lon = groups * group + within
            here = (k.l >> 5) == group
            a = turn(x_refs[0][pl.ds(lon, block, stride=lons), :], HALO * group)
            b = turn(x_refs[-1][pl.ds(lon, block, stride=lons), :], HALO * group - (LANES - HALO))
            to_left = a if to_left is None else jnp.where(here, a, to_left)
            to_right = b if to_right is None else jnp.where(here, b, to_right)
        to_left_ref[within] = to_left
        to_right_ref[within, at, :] = to_right

    @pl.when(pl.program_id(0) == 0)
    def _():
        members = to_right_ref.shape[1] - SUB
        for within in range(groups):
            to_right_ref[within, pl.ds(members, SUB), :] = table_ref[...]


def weights_kernel(index_ref, table_ref, halo_ref, out_ref, arranged_ref):
    l = lax.broadcasted_iota(jnp.int32, (SUB, LANES), 1)
    block = out_ref.shape[1]
    table = get(table_ref, 0, table_ref.shape[1] // LANES)
    halo = jnp.where(l >= LANES - 16, halo_ref[0], 0.0)
    for level in range(LEVELS):
        scale = tap_1 ** (4 * (level + 1))
        mains = MAINS[level]
        stride = 2 << level
        count = 64 * len(table) >> level
        step = LANES // stride
        start, size = 0 * l, count * 2
        for bit in range(min(level + 1, 3)):
            size = size // 2
            start = start + size * ((l >> bit) & 1)
        for j in range(mains):
            k = (start + step * j + l // stride) << level
            value = jnp.zeros((SUB, LANES), jnp.float32)
            for v in range(len(table)):
                value = jnp.where((k >> 7) == v, pick(table[v], k & 127), value)
            arranged_ref[j] = value * scale
        edge = pick(halo, 64 + (l >> 1))
        arranged_ref[mains] = jnp.where(l >= LANES - 2 * stride, edge, 0.0) * scale
        for band in range(3 if level < LEVELS - 1 else 4):
            table_row = index_ref[3 * level + band]
            for i in range(mains + 1):
                out_ref[WEIGHTS[level, band] + i] = jnp.broadcast_to(
                    arranged_ref[i, pl.ds(table_row, 1), :], (block, LANES)
                )


def send_kernel(lons, block, x_refs, left_ref, right_ref, c1_ref, to_right, to_left, far_right, far_left):
    k = Lanes(block)
    many = Stacks(block)
    half = lons // 2
    edges_right, edges_left = [k.zero, k.zero], [k.zero]

    def rows(i):
        return pair(
            read_row(x_refs, left_ref, right_ref, 2 * i, lons, k),
            read_row(x_refs, left_ref, right_ref, 2 * i + 1, lons, k),
        )

    c1 = [None] * half
    h0b = b_next = None
    for start in reversed(range(0, half, SEND_STACK)):
        coarse = []
        pairs0 = [rows(i) for i in range(start, start + SEND_STACK)]
        for i in range(start, start + SEND_STACK):
            a = pairs0[i - start][0]
            if i == half - 1:
                k.fill(edges_right, "a0", a[-1])
                coarse.append(a)
            else:
                after = pairs0[i - start + 1][1] if i < start + SEND_STACK - 1 else b_next
                coarse.append(plus(a, after, Q))
        if start == 0:
            coarse.append(pairs0[0][1])
            k.fill(edges_left, "b0", coarse[-1][-1])
        coarse = many.low(coarse, 0)
        c1[start : start + SEND_STACK] = coarse[:SEND_STACK]
        if start == 0:
            h0b = coarse[-1]
        b_next = pairs0[0][1]
    for i in range(half - 1):
        put(c1_ref, 5 * i, c1[i])

    def message(ref, places, edges, item, row):
        put(ref, places[item], row[:-1])
        k.fill(edges, item, row[-1])

    message(to_right, RIGHT, edges_right, "c1", c1[half - 2])
    pairs1 = [pair(c1[2 * i], c1[2 * i + 1]) for i in range(half // 2)]
    message(to_right, RIGHT, edges_right, "a1", pairs1[-2][0])
    b1 = pairs1[0][1]
    message(to_left, LEFT, edges_left, "b1", b1)

    def lows(pairs, level):
        rows = [plus(pairs[i][0], pairs[i + 1][1], Q) for i in range(len(pairs) - 1)] + [pairs[-1][0]]
        return many.low(rows, level)

    c2 = lows(pairs1, 1)
    pairs2 = [pair(c2[2 * i], c2[2 * i + 1]) for i in range(half // 4)]
    message(to_right, RIGHT, edges_right, "a2", pairs2[-2][0])
    b2 = pairs2[0][1]
    message(to_left, LEFT, edges_left, "b2", b2)
    c3 = lows(pairs2, 2)
    a3, b3 = pair(c3[0], c3[1])
    put(far_right, 0, a3)
    message(to_left, LEFT, edges_left, "b3", b3)

    d1 = times(Q, h0b)
    d2 = many.low([times(Q * T, d1), plus(d1, b1, Q)], 1)
    da, db = pair(d2[0], d2[1])
    d3 = many.low([times(Q, db), plus(da, b2, Q)], 2)
    ka, kb = pair(d3[0], d3[1])
    message(to_right, RIGHT, edges_right, "k", ka)
    put(far_left, 0, kb)
    put(to_right, RIGHT["edge"], edges_right)
    put(to_left, LEFT["edge"], edges_left)


def inner_kernel(lons, block, w_ref, x_refs, left_ref, right_ref, out_ref):
    k = Lanes(block)
    half = lons // 2

    def weight(band):
        return [w_ref[WEIGHTS[0, band] + i] for i in range(5)]

    def store(p, a, b):
        y0, y1 = unpair(a, b)
        put(out_ref, 2 * p * len(a), y0)
        put(out_ref, (2 * p + 1) * len(a), y1)

    def rows(i):
        return pair(
            read_row(x_refs, left_ref, right_ref, 2 * i, lons, k),
            read_row(x_refs, left_ref, right_ref, 2 * i + 1, lons, k),
        )

    many = Stacks(block)
    a, _ = rows(0)
    before = [k.zero] * (len(a) - 1)
    for start in range(0, half - 1, INNER_STACK):
        count = min(INNER_STACK, half - 1 - start)
        lows, highs = [], []
        for p in range(start, start + count):
            a_next, b_next = rows(p + 1)
            lows.append(plus(a, b_next, Q))
            highs.append(plus(b_next, a, -Q))
            a = a_next
        h, g = many.analyze(highs + lows, 0)
        a_sum, b_sum = [], []
        for n in range(count):
            hh, hg, lg = mul(h[n], weight(1)), mul(g[n], weight(2)), mul(g[count + n], weight(0))
            a_sum.append(plus(hh, hg, -Q))
            b_sum.append(plus(hg, hh, Q))
            a_sum.append(times(-Q, lg))
            b_sum.append(lg)
        joined = many.join(a_sum, b_sum, 0)
        for n in range(count):
            z, y = joined[2 * n : 2 * n + 2]
            store(start + n, plus(y, z, -Q), before)
            before = plus(z, y, Q)
    store(half - 1, [k.zero] * len(before), before)


def outer_kernel(
    lons,
    block,
    w_ref,
    part_ref,
    c1_ref,
    own_a,
    own_b,
    own_right,
    own_left,
    left_a,
    right_b,
    from_left,
    from_right,
    far_left,
    far_right,
    out_ref,
    y_ref,
):
    many = Stacks(block)
    half = lons // 2

    def edge(ref, name, places):
        at, by, _ = EDGE[name]
        return turn(get(ref, places["edge"] + at, 1)[0], -by)

    def item(ref, name, places):
        return get(ref, places[name], COUNT[name]) + [edge(ref, name, places)]

    def weight(level, band):
        return [w_ref[WEIGHTS[level, band] + i] for i in range(MAINS[level] + 1)]

    def inner(level, rows, a_first, b_last):
        pairs = [pair(rows[2 * i], rows[2 * i + 1]) for i in range(len(rows) // 2)]
        a = [a_first] + [p[0] for p in pairs]
        b = [p[1] for p in pairs] + [b_last]
        n = len(a)
        h, g = many.analyze(
            [plus(j, i, -Q) for i, j in zip(a, b)] + [plus(i, j, Q) for i, j in zip(a, b)], level
        )
        highs = [
            (mul(h[i], weight(level, 1)), mul(g[i], weight(level, 2))) for i in range(n)
        ]
        return h[n:], [mul(g[n + i], weight(level, 0)) for i in range(n)], highs

    def outer(level, coarse, band_0, highs):
        n = len(coarse)
        rows = many.synthesize(coarse + [h[0] for h in highs], band_0 + [h[1] for h in highs], level)
        a = [plus(rows[i], rows[n + i], -Q) for i in range(n)]
        b = [plus(rows[n + i], rows[i], Q) for i in range(n)]
        field = []
        for i in range(1, n):
            field.extend(unpair(a[i], b[i - 1]))
        return field

    count = own_a.shape[1] // LANES
    a_first = get(left_a, 0, count) + [edge(from_left, "a0", RIGHT)]
    b_first = get(own_b, 0, count) + [edge(own_left, "b0", LEFT)]
    a_last = get(own_a, 0, count) + [edge(own_right, "a0", RIGHT)]
    b_last = get(right_b, 0, count) + [edge(from_right, "b0", LEFT)]
    h, g = many.analyze(
        [plus(a_first, b_first, Q), plus(a_last, b_last, Q), plus(b_first, a_first, -Q), plus(b_last, a_last, -Q)], 0
    )
    g_first, g_last = mul(g[0], weight(0, 0)), mul(g[1], weight(0, 0))
    straddling = [(mul(h[i], weight(0, 1)), mul(g[i], weight(0, 2))) for i in (2, 3)]

    c1 = [item(from_left, "c1", RIGHT), h[0]]
    c1 += [get(c1_ref, 5 * i, 5) for i in range(half - 1)]
    c1.append(h[1])
    c2, g1, z1 = inner(1, c1, item(from_left, "a1", RIGHT), item(from_right, "b1", LEFT))
    c3, g2, z2 = inner(2, c2, item(from_left, "a2", RIGHT), item(from_right, "b2", LEFT))
    a3 = plus(get(far_left, 0, 2), item(from_left, "k", RIGHT))
    b3 = plus(item(from_right, "b3", LEFT), get(far_right, 0, 2))
    c4, g3, z3 = inner(3, c3, a3, b3)
    field = [mul(c, weight(3, 3)) for c in c4]
    for level, g_rows, z_rows in ((3, g3, z3), (2, g2, z2), (1, g1, z1)):
        field = outer(level, field, g_rows, z_rows)
    field = field[1:]

    a_rows, b_rows = list(field), [times(Q, f) for f in field]
    a_rows[0], b_rows[0] = plus(field[0], g_first, -Q), plus(g_first, field[0], Q)
    a_rows[-1], b_rows[-1] = plus(field[-1], g_last, -Q), plus(g_last, field[-1], Q)
    for hh, hg in straddling:
        a_rows.append(plus(hh, hg, -Q))
        b_rows.append(plus(hg, hh, Q))
    joined = []
    for start in range(0, len(a_rows), OUTER_STACK):
        joined += many.join(a_rows[start : start + OUTER_STACK], b_rows[start : start + OUTER_STACK], 0)
    low, (z_first, z_last) = joined[: half + 1], joined[half + 1 :]

    b = plus(z_first, low[0], Q)
    for p in range(half):
        if p < half - 1:
            a = low[p + 1]
            b_next = times(Q, a)
        else:
            a = plus(low[p + 1], z_last, -Q)
        for j, y in enumerate(unpair(a, b)):
            part = get(part_ref, (2 * p + j) * len(y), len(y))
            for v in range(len(y)):
                y_ref[v, pl.ds(block * (2 * p + j), block), :] = part[v] + y[v]
        b = b_next
    for v in range(y_ref.shape[0]):
        for member in range(block):
            out_ref[pl.ds(lons * member, lons), pl.ds(LANES * v, LANES)] = y_ref[
                v, pl.ds(member, lons, stride=block), :
            ]


def shift(x, axis, by, cyclic):
    size = lax.axis_size(axis)
    if cyclic:
        pairs = [(i, (i + by) % size) for i in range(size)]
    else:
        pairs = [(i, i + by) for i in range(size) if 0 <= i + by < size]
    return lax.ppermute(x, axis, pairs)


def per_device(perturbation, weight_table, band_index):
    members, lons, lats = perturbation.shape
    assert lons == 16 and lats == 8 * LANES and members % BLOCK == 0
    block = BLOCK
    steps = members // block
    x = perturbation.reshape(members * lons, lats)
    shape = lambda *dims: jax.ShapeDtypeStruct(dims, jnp.float32)
    groups = lons // 4
    cols = lats // LANES
    params = pltpu.CompilerParams(vmem_limit_bytes=60 * 1024 * 1024)
    by_member = lambda width: pl.BlockSpec((block, width), lambda i: (i, 0))
    x_specs = [pl.BlockSpec((block * lons, LANES), lambda i, v=v: (i, v)) for v in range(cols)]
    halo_spec = pl.BlockSpec((groups, block, LANES), lambda i: (0, i, 0))
    w_spec = pl.BlockSpec((WEIGHT_COUNT, block, LANES), lambda i: (0, 0, 0))

    to_left, to_right, own_a, own_b = pl.pallas_call(
        lambda *refs: first_kernel(lons, block, refs[:cols], *refs[cols:]),
        grid=(steps,),
        in_specs=x_specs + [pl.BlockSpec((SUB, LANES), lambda i: (0, lats // 2 // LANES - 1))],
        out_specs=[
            halo_spec,
            pl.BlockSpec((groups, members + SUB, LANES), lambda i: (0, 0, 0)),
            by_member(lats),
            by_member(lats),
        ],
        out_shape=[
            shape(groups, members, LANES),
            shape(groups, members + SUB, LANES),
            shape(members, lats),
            shape(members, lats),
        ],
        compiler_params=params,
        name="first",
    )(*[x] * cols, weight_table)
    before = shift(to_right, "lat", 1, False)
    beyond = shift(to_left, "lat", -1, False)
    left_a = shift(own_a, "lon", 1, True)
    right_b = shift(own_b, "lon", -1, True)

    weights = pl.pallas_call(
        weights_kernel,
        grid=(1,),
        in_specs=[
            pl.BlockSpec(memory_space=pltpu.SMEM),
            pl.BlockSpec((SUB, lats // 2), lambda i: (0, 0)),
            pl.BlockSpec((1, SUB, LANES), lambda i: (0, members // SUB, 0)),
        ],
        out_specs=pl.BlockSpec((WEIGHT_COUNT, block, LANES), lambda i: (0, 0, 0)),
        out_shape=shape(WEIGHT_COUNT, block, LANES),
        scratch_shapes=[pltpu.VMEM((5, SUB, LANES), jnp.float32)],
        compiler_params=params,
        name="weights",
    )(band_index, weight_table, before)

    c1_width = (lons // 2 - 1) * 5 * LANES
    right_width, left_width = RIGHT_SIZE * LANES, LEFT_SIZE * LANES
    c1, to_right, to_left, far_right, far_left = pl.pallas_call(
        lambda *refs: send_kernel(lons, block, refs[:cols], *refs[cols:]),
        grid=(steps,),
        in_specs=x_specs + [halo_spec, halo_spec],
        out_specs=[by_member(c1_width), by_member(right_width), by_member(left_width)] + [by_member(2 * LANES)] * 2,
        out_shape=[
            shape(members, c1_width),
            shape(members, right_width),
            shape(members, left_width),
            shape(members, 2 * LANES),
            shape(members, 2 * LANES),
        ],
        compiler_params=params,
        cost_estimate=pl.CostEstimate(flops=10**7, bytes_accessed=10**7, transcendentals=0),
        name="send",
    )(*[x] * cols, before, beyond)
    from_left = shift(to_right, "lon", 1, True)
    from_right = shift(to_left, "lon", -1, True)
    from_far_left = shift(far_right, "lon", 2, True)
    from_far_right = shift(far_left, "lon", -2, True)

    part = pl.pallas_call(
        lambda *refs: inner_kernel(lons, block, refs[0], refs[1 : cols + 1], *refs[cols + 1 :]),
        grid=(steps,),
        in_specs=[w_spec] + x_specs + [halo_spec, halo_spec],
        out_specs=by_member(lons * lats),
        out_shape=shape(members, lons * lats),
        compiler_params=params,
        cost_estimate=pl.CostEstimate(flops=10**7, bytes_accessed=4 * 10**7, transcendentals=0),
        name="inner",
    )(weights, *[x] * cols, before, beyond)

    out = pl.pallas_call(
        lambda *refs: outer_kernel(lons, block, *refs),
        grid=(steps,),
        in_specs=[w_spec, by_member(lons * lats), by_member(c1_width), by_member(lats), by_member(lats)]
        + [by_member(right_width), by_member(left_width), by_member(lats), by_member(lats)]
        + [by_member(right_width), by_member(left_width)]
        + [by_member(2 * LANES)] * 2,
        out_specs=pl.BlockSpec((block * lons, lats), lambda i: (i, 0)),
        out_shape=shape(members * lons, lats),
        scratch_shapes=[pltpu.VMEM((cols, block * lons, LANES), jnp.float32)],
        compiler_params=params,
        name="outer",
    )(
        weights,
        part,
        c1,
        own_a,
        own_b,
        to_right,
        to_left,
        left_a,
        right_b,
        from_left,
        from_right,
        from_far_left,
        from_far_right,
    )
    return out.reshape(members, lons, lats)


def solution(mesh):
    placed = (P(None, "lon", "lat"), P(None, "lat"), P())

    return jax.shard_map(per_device, mesh=mesh, in_specs=placed, out_specs=P(None, "lon", "lat"), check_vma=False)
```

profile of v0, /device:TPU:1, one launch (start us, length us, event | category | flops | bytes accessed | tf_op | source)
XLA Modules:
  0.0 74.5 jit_solution(12775279661890396830)
XLA Ops:
  0.0 3.9 %first.1 = (f32[4,80,128]{2,1,0:T(8,128)}, f32[4,88,128]{2,1,0:T(8,128)}, f32[80,1024]{1,0:T(8,128)}, f32[80,1024]{1,0:T(8,128)}) custom-call(f32[1280,1024]{1,0:T(8,128)} %bitcast.2, f32[1280,1024]{1,0:T(8,128)} %bitcast.3, f32[1280,1024]{1,0:T(8,128)} %bitcast.4, f32[1280,1024]{1,0:T(8,128)} %bitcast.5, f32[1280,1024]{1,0:T(8,128)} %bitcast.6, ...), custom_call_target="tpu_custom_call" | custom-call | tf_op jit(solution)/shard_map/first/pallas_call | solution.py:528
  3.9 4.5 %collective-permute-start = (f32[4,88,128]{2,1,0:T(8,128)}, f32[4,88,128]{2,1,0:T(8,128)S(1)}, u32[]{:S(2)}, u32[]{:S(2)}) collective-permute-start(f32[4,88,128]{2,1,0:T(8,128)} %get-tuple-element.14), channel_id=1, source_target_pairs={{0,1},{1,2},{2,3},{4,5},{5,6},{6,7},{8,9},{9,10},{10,11},{12,13},{... | collective-permute-start | bytes 540680 | tf_op jit(solution)/shard_map/ppermute | solution.py:510
  8.4 0.0 copy-start.3
  8.5 0.0 copy-start.4
  8.5 2.1 %collective-permute-start.1 = (f32[4,80,128]{2,1,0:T(8,128)}, f32[4,80,128]{2,1,0:T(8,128)S(1)}, u32[]{:S(2)}, u32[]{:S(2)}) collective-permute-start(f32[4,80,128]{2,1,0:T(8,128)} %get-tuple-element.15), channel_id=1, source_target_pairs={{1,0},{2,1},{3,2},{5,4},{6,5},{7,6},{9,8},{10,9},{11,10},{13,12},{... | collective-permute-start | bytes 491528 | tf_op jit(solution)/shard_map/ppermute | solution.py:510
  10.5 4.9 %collective-permute-done.1.refs_10_.refs_9_ = f32[4,80,128]{2,1,0:T(8,128)S(1)} collective-permute-done((f32[4,80,128]{2,1,0:T(8,128)}, f32[4,80,128]{2,1,0:T(8,128)S(1)}, u32[]{:S(2)}, u32[]{:S(2)}) %collective-permute-start.1) | collective-permute-done | bytes 163872 | tf_op jit(solution)/shard_map/ppermute | solution.py:510
  15.4 0.0 copy-start.1
  15.4 0.0 collective-permute-done.halo_ref.refs_9_.refs_8_
  15.5 0.7 copy-done.1
  16.1 0.0 copy-start
  16.1 0.7 copy-done
  16.8 7.1 %send.1 = (f32[80,4480]{1,0:T(8,128)}, f32[80,1664]{1,0:T(8,128)}, f32[80,1024]{1,0:T(8,128)}, f32[80,256]{1,0:T(8,128)}, f32[80,256]{1,0:T(8,128)}) custom-call(f32[1280,1024]{1,0:T(8,128)} %bitcast.13, f32[1280,1024]{1,0:T(8,128)} %bitcast.11, f32[1280,1024]{1,0:T(8,128)} %bitcast.12, f32[1280,1024]{1,0:T(8,128)} %bitcast.10, f32[1280,1024]{1,0:T(8,128)} %bitcast.14, ...), custom_call_target="tpu_custom_call" | custom-call | flops 10000000 | bytes 10000000 | tf_op jit(solution)/shard_map/send/pallas_call | solution.py:569
  23.9 1.3 %collective-permute-start.4 = (f32[80,1664]{1,0:T(8,128)}, f32[80,1664]{1,0:T(8,128)S(1)}, u32[]{:S(2)}, u32[]{:S(2)}) collective-permute-start(f32[80,1664]{1,0:T(8,128)} %get-tuple-element.19.refs_5_), channel_id=1, source_target_pairs={{0,4},{4,8},{8,12},{12,16},{16,20},{20,24},{24,28},{28,0},{1,5},{5... | collective-permute-start | bytes 1597448 | tf_op jit(solution)/shard_map/ppermute | solution.py:510
  25.2 0.0 copy-done.3
  25.2 1.2 %collective-permute-start.2 = (f32[80,1024]{1,0:T(8,128)S(1)}, f32[80,1024]{1,0:T(8,128)S(1)}, u32[]{:S(2)}, u32[]{:S(2)}) collective-permute-start(f32[80,1024]{1,0:T(8,128)S(1)} %copy-done.3), channel_id=1, source_target_pairs={{0,4},{4,8},{8,12},{12,16},{16,20},{20,24},{24,28},{28,0},{1,5},{5... | collective-permute-start | bytes 983048 | tf_op jit(solution)/shard_map/ppermute | solution.py:510
  26.5 0.0 copy-done.4
  26.5 2.9 %collective-permute-start.3 = (f32[80,1024]{1,0:T(8,128)S(1)}, f32[80,1024]{1,0:T(8,128)S(1)}, u32[]{:S(2)}, u32[]{:S(2)}) collective-permute-start(f32[80,1024]{1,0:T(8,128)S(1)} %copy-done.4), channel_id=1, source_target_pairs={{0,28},{4,0},{8,4},{12,8},{16,12},{20,16},{24,20},{28,24},{1,29},{... | collective-permute-start | bytes 983048 | tf_op jit(solution)/shard_map/ppermute | solution.py:510
  29.4 0.4 collective-permute-start.5
  29.8 0.0 collective-permute-start.6
  29.8 15.6 %collective-permute-done.6.refs_11_ = f32[80,256]{1,0:T(8,128)S(1)} collective-permute-done((f32[80,256]{1,0:T(8,128)}, f32[80,256]{1,0:T(8,128)S(1)}, u32[]{:S(2)}, u32[]{:S(2)}) %collective-permute-start.6) | collective-permute-done | bytes 81952 | tf_op jit(solution)/shard_map/ppermute | solution.py:510
  45.4 0.0 copy-start.8
  45.4 2.0 %collective-permute-start.7 = (f32[80,256]{1,0:T(8,128)}, f32[80,256]{1,0:T(8,128)S(1)}, u32[]{:S(2)}, u32[]{:S(2)}) collective-permute-start(f32[80,256]{1,0:T(8,128)} %get-tuple-element.22), channel_id=1, source_target_pairs={{0,24},{4,28},{8,0},{12,4},{16,8},{20,12},{24,16},{28,20},{1,25},{... | collective-permute-start | bytes 245768 | tf_op jit(solution)/shard_map/ppermute | solution.py:510
  47.4 1.8 %weights.1.refs_0_ = f32[38,40,128]{2,1,0:T(8,128)} custom-call(s32[13]{0:T(128)} %index_ref.1, f32[8,512]{1,0:T(8,128)} %table_ref.1, f32[4,88,128]{2,1,0:T(8,128)} %copy-done), custom_call_target="tpu_custom_call" | custom-call | tf_op jit(solution)/shard_map/weights/pallas_call | solution.py:552
  49.2 10.4 %inner.1.refs_1_ = f32[80,16384]{1,0:T(8,128)} custom-call(f32[38,40,128]{2,1,0:T(8,128)} %weights.1.refs_0_, f32[1280,1024]{1,0:T(8,128)} %bitcast.18, f32[1280,1024]{1,0:T(8,128)} %bitcast.19, f32[1280,1024]{1,0:T(8,128)} %bitcast.20, f32[1280,1024]{1,0:T(8,128)} %bitcast.21, f32[1280,1024]{1,0:T(8,128)} %bitcast.22, f32[1280,1024]{1,0:T(8,128)} %bitcast.23, ...), custom_call_target="tpu_custom_call" | custom-call | flops 10000000 | bytes 40000000 | tf_op jit(solution)/shard_map/inner/pallas_call | solution.py:590
  59.6 0.0 copy-done.8
  59.6 0.0 collective-permute-done.7.refs_12_
  59.6 0.0 copy-start.9
  59.6 0.0 collective-permute-done.2.refs_7_
  59.6 0.0 copy-start.5
  59.6 0.0 collective-permute-done.3.refs_8_
  59.6 0.0 copy-start.6
  59.6 0.0 collective-permute-done.5.refs_10_
  59.7 0.0 copy-start.7
  59.7 0.0 collective-permute-done.4.refs_9_
  59.7 0.0 copy-start.2
  59.7 0.5 copy-done.9
  60.2 0.1 copy-done.5
  60.4 0.1 copy-done.6
  60.5 0.1 copy-done.7
  60.6 0.2 copy-done.2
  60.8 13.7 %outer.1 = f32[1280,1024]{1,0:T(8,128)} custom-call(f32[38,40,128]{2,1,0:T(8,128)} %weights.1.refs_0_, f32[80,16384]{1,0:T(8,128)} %inner.1.refs_1_, f32[80,4480]{1,0:T(8,128)} %get-tuple-element.16.refs_2_, f32[80,1024]{1,0:T(8,128)} %get-tuple-element.17.refs_3_, f32[80,1024]{1,0:T(8,128)} %get-tuple-element.18.refs_4_, ...), custom_call_target="tpu_custom_call" | custom-call | tf_op jit(solution)/shard_map/outer/pallas_call | solution.py:601
Async XLA Ops:
  3.9 11.5 %collective-permute-start = (f32[4,88,128]{2,1,0:T(8,128)}, f32[4,88,128]{2,1,0:T(8,128)S(1)}, u32[]{:S(2)}, u32[]{:S(2)}) collective-permute-start(f32[4,88,128]{2,1,0:T(8,128)} %get-tuple-element.14), channel_id=1, source_target_pairs={{0,1},{1,2},{2,3},{4,5},{5,6},{6,7},{8,9},{9,10},{10,11},{12,13},{... | collective-permute-start | bytes 540680 | tf_op jit(solution)/shard_map/ppermute | solution.py:510
  8.4 16.8 %copy-start.3 = (f32[80,1024]{1,0:T(8,128)S(1)}, f32[80,1024]{1,0:T(8,128)}, u32[]{:S(2)}) copy-start(f32[80,1024]{1,0:T(8,128)} %get-tuple-element.17.refs_3_) | copy-start | bytes 983044
  8.5 18.0 %copy-start.4 = (f32[80,1024]{1,0:T(8,128)S(1)}, f32[80,1024]{1,0:T(8,128)}, u32[]{:S(2)}) copy-start(f32[80,1024]{1,0:T(8,128)} %get-tuple-element.18.refs_4_) | copy-start | bytes 983044
  8.5 7.0 %collective-permute-start.1 = (f32[4,80,128]{2,1,0:T(8,128)}, f32[4,80,128]{2,1,0:T(8,128)S(1)}, u32[]{:S(2)}, u32[]{:S(2)}) collective-permute-start(f32[4,80,128]{2,1,0:T(8,128)} %get-tuple-element.15), channel_id=1, source_target_pairs={{1,0},{2,1},{3,2},{5,4},{6,5},{7,6},{9,8},{10,9},{11,10},{13,12},{... | collective-permute-start | bytes 491528 | tf_op jit(solution)/shard_map/ppermute | solution.py:510
  15.4 0.7 copy-start.1
  16.1 0.7 copy-start
  23.9 35.7 %collective-permute-start.4 = (f32[80,1664]{1,0:T(8,128)}, f32[80,1664]{1,0:T(8,128)S(1)}, u32[]{:S(2)}, u32[]{:S(2)}) collective-permute-start(f32[80,1664]{1,0:T(8,128)} %get-tuple-element.19.refs_5_), channel_id=1, source_target_pairs={{0,4},{4,8},{8,12},{12,16},{16,20},{20,24},{24,28},{28,0},{1,5},{5... | collective-permute-start | bytes 1597448 | tf_op jit(solution)/shard_map/ppermute | solution.py:510
  25.2 34.4 %collective-permute-start.2 = (f32[80,1024]{1,0:T(8,128)S(1)}, f32[80,1024]{1,0:T(8,128)S(1)}, u32[]{:S(2)}, u32[]{:S(2)}) collective-permute-start(f32[80,1024]{1,0:T(8,128)S(1)} %copy-done.3), channel_id=1, source_target_pairs={{0,4},{4,8},{8,12},{12,16},{16,20},{20,24},{24,28},{28,0},{1,5},{5... | collective-permute-start | bytes 983048 | tf_op jit(solution)/shard_map/ppermute | solution.py:510
  26.5 33.1 %collective-permute-start.3 = (f32[80,1024]{1,0:T(8,128)S(1)}, f32[80,1024]{1,0:T(8,128)S(1)}, u32[]{:S(2)}, u32[]{:S(2)}) collective-permute-start(f32[80,1024]{1,0:T(8,128)S(1)} %copy-done.4), channel_id=1, source_target_pairs={{0,28},{4,0},{8,4},{12,8},{16,12},{20,16},{24,20},{28,24},{1,29},{... | collective-permute-start | bytes 983048 | tf_op jit(solution)/shard_map/ppermute | solution.py:510
  29.4 30.2 %collective-permute-start.5 = (f32[80,1024]{1,0:T(8,128)}, f32[80,1024]{1,0:T(8,128)S(1)}, u32[]{:S(2)}, u32[]{:S(2)}) collective-permute-start(f32[80,1024]{1,0:T(8,128)} %get-tuple-element.20.refs_6_), channel_id=1, source_target_pairs={{0,28},{4,0},{8,4},{12,8},{16,12},{20,16},{24,20},{28,24},{1,29},{... | collective-permute-start | bytes 983048 | tf_op jit(solution)/shard_map/ppermute | solution.py:510
  29.8 15.6 %collective-permute-start.6 = (f32[80,256]{1,0:T(8,128)}, f32[80,256]{1,0:T(8,128)S(1)}, u32[]{:S(2)}, u32[]{:S(2)}) collective-permute-start(f32[80,256]{1,0:T(8,128)} %get-tuple-element.21), channel_id=1, source_target_pairs={{0,8},{4,12},{8,16},{12,20},{16,24},{20,28},{24,0},{28,4},{1,9},{5... | collective-permute-start | bytes 245768 | tf_op jit(solution)/shard_map/ppermute | solution.py:510
  45.4 14.2 %copy-start.8 = (f32[80,256]{1,0:T(8,128)}, f32[80,256]{1,0:T(8,128)S(1)}, u32[]{:S(2)}) copy-start(f32[80,256]{1,0:T(8,128)S(1)} %collective-permute-done.6.refs_11_) | copy-start | bytes 245764
  45.4 14.2 %collective-permute-start.7 = (f32[80,256]{1,0:T(8,128)}, f32[80,256]{1,0:T(8,128)S(1)}, u32[]{:S(2)}, u32[]{:S(2)}) collective-permute-start(f32[80,256]{1,0:T(8,128)} %get-tuple-element.22), channel_id=1, source_target_pairs={{0,24},{4,28},{8,0},{12,4},{16,8},{20,12},{24,16},{28,20},{1,25},{... | collective-permute-start | bytes 245768 | tf_op jit(solution)/shard_map/ppermute | solution.py:510
  59.6 0.6 copy-start.9
  59.6 0.8 %copy-start.5 = (f32[80,1024]{1,0:T(8,128)}, f32[80,1024]{1,0:T(8,128)S(1)}, u32[]{:S(2)}) copy-start(f32[80,1024]{1,0:T(8,128)S(1)} %collective-permute-done.2.refs_7_) | copy-start | bytes 983044
  59.6 0.8 %copy-start.6 = (f32[80,1024]{1,0:T(8,128)}, f32[80,1024]{1,0:T(8,128)S(1)}, u32[]{:S(2)}) copy-start(f32[80,1024]{1,0:T(8,128)S(1)} %collective-permute-done.3.refs_8_) | copy-start | bytes 983044
  59.7 0.9 %copy-start.7 = (f32[80,1024]{1,0:T(8,128)}, f32[80,1024]{1,0:T(8,128)S(1)}, u32[]{:S(2)}) copy-start(f32[80,1024]{1,0:T(8,128)S(1)} %collective-permute-done.5.refs_10_) | copy-start | bytes 983044
  59.7 1.1 %copy-start.2 = (f32[80,1664]{1,0:T(8,128)}, f32[80,1664]{1,0:T(8,128)S(1)}, u32[]{:S(2)}) copy-start(f32[80,1664]{1,0:T(8,128)S(1)} %collective-permute-done.4.refs_9_) | copy-start | bytes 1597444
where the time goes:
time: 75.2 us; the launch traced here: 74.5 us
  Pallas kernels  36.9 us (49%)
  waiting for transfers between devices  20.5 us (27%)
  starting transfers between devices  14.4 us (19%)
  local copies, waits for them, and re-layouts  2.49 us (3%)
    ppermute x8, waiting for transfers between devices, shift(): return lax.ppermute(x, axis, pairs)  20.5 us
    ppermute x8, starting transfers between devices, shift(): return lax.ppermute(x, axis, pairs)  14.4 us
    pallas_call x1, Pallas kernels, per_device(): pl.pallas_call(lambda *refs: outer_kernel(lons, block, *refs), grid=(step...  13.7 us
    pallas_call x1, Pallas kernels, per_device(): pl.pallas_call(lambda *refs: inner_kernel(lons, block, refs[0], refs[1:co...  10.4 us
    pallas_call x1, Pallas kernels, per_device(): pl.pallas_call(lambda *refs: send_kernel(lons, block, refs[:cols], *refs[...  7.13 us
    pallas_call x1, Pallas kernels, per_device(): pl.pallas_call(lambda *refs: first_kernel(lons, block, refs[:cols], *refs...  3.94 us
    unnamed x20, local copies, waits for them, and re-layouts  2.49 us
    pallas_call x1, Pallas kernels, per_device(): pl.pallas_call(weights_kernel, grid=(1,), in_specs=[pl.BlockSpec(memory_s...  1.79 us
  transfers between devices with their start and end apart: 8, of which 2 were waited for; matrix products, arithmetic and copies ran while one was open for 0% of the time, Pallas kernels for 16%

commit v1 on v0

--- a/solution.py
+++ b/solution.py
@@ -11,7 +11,10 @@
 LEVELS = 4
 LANES = 128
 SUB = 8
-BLOCK = 40
+FIRST_BLOCK = 40
+SEND_BLOCK = 40
+INNER_BLOCK = 40
+OUTER_BLOCK = 40
 SEND_STACK = 4
 INNER_STACK = 2
 OUTER_STACK = 6
@@ -62,6 +65,7 @@
 class Lanes:
     def __init__(self, rows):
         l = lax.broadcasted_iota(jnp.int32, (rows, LANES), 1)
+        self.rows = rows
         self.l = l
         self.zero = jnp.zeros((rows, LANES), jnp.float32)
         self.bit = [(l & (1 << level)) == 0 for level in range(LEVELS)]
@@ -197,46 +201,76 @@
     return plus(b, a, -T), plus(a, b, T)
 
 
-def read_row(x_refs, left_ref, right_ref, lon, lons, k):
-    rows = k.l.shape[0]
-    row = [x_ref[pl.ds(lon, rows, stride=lons), :] for x_ref in x_refs]
+class View:
+    def __init__(self, ref, block):
+        self.ref = ref
+        self.block = block
+
+    def rows(self):
+        return pl.ds(pl.multiple_of(pl.program_id(0) * self.block, self.block), self.block)
+
+    def put(self, at, values):
+        for i, v in enumerate(values):
+            self.ref[at + i, self.rows(), :] = v
+
+    def get(self, at, count):
+        return [self.ref[at + i, self.rows(), :] for i in range(count)]
+
+
+def views(block, refs):
+    return [View(ref, block) for ref in refs]
+
+
+def weight_of(w_ref, block, level, band):
+    at = WEIGHTS[level, band]
+    return [jnp.concatenate([w_ref[at + i]] * (block // SUB), 0) for i in range(MAINS[level] + 1)]
+
+
+def put(view, at, values):
+    view.put(at, values)
+
+
+def get(view, at, count):
+    return view.get(at, count)
+
+
+def read_row(x_view, left_view, right_view, lon, lons, k):
+    cols = x_view.ref.shape[0] // lons
+    row = x_view.get(lon * cols, cols)
     group, within = divmod(lon, lons // 4)
-    beyond = turn(right_ref[within], -HALO * group)
-    before = turn(left_ref[within], LANES - HALO - HALO * group)
+    beyond = turn(right_view.get(within, 1)[0], -HALO * group)
+    before = turn(left_view.get(within, 1)[0], LANES - HALO - HALO * group)
     row.append(jnp.where(k.l < LANES // 2, beyond, before))
     return row
 
 
-def put(ref, at, values):
-    for i, v in enumerate(values):
-        ref[:, pl.ds(LANES * (at + i), LANES)] = v
-
-
-def get(ref, at, count):
-    return [ref[:, pl.ds(LANES * (at + i), LANES)] for i in range(count)]
-
-
-def first_kernel(lons, block, x_refs, table_ref, to_left_ref, to_right_ref, a_ref, b_ref):
+def first_kernel(lons, block, x_refs, table_ref, x_out, to_left_ref, to_right_ref, a_ref, b_ref):
     k = Lanes(block)
+    x_out, to_left_out, to_right_out, a_out, b_out = views(block, (x_out, to_left_ref, to_right_ref, a_ref, b_ref))
     groups = lons // 4
-
-    def row(lon):
-        return [x_ref[pl.ds(lon, block, stride=lons), :] for x_ref in x_refs]
-
-    put(b_ref, 0, pair(row(0), row(1))[1])
-    put(a_ref, 0, pair(row(lons - 2), row(lons - 1))[0])
-    at = pl.ds(pl.multiple_of(pl.program_id(0) * block, block), block)
+    cols = len(x_refs)
+    edges = []
+    kept = {}
+    for lon in range(lons):
+        row = [x_ref[pl.ds(lon, block, stride=lons), :] for x_ref in x_refs]
+        x_out.put(lon * cols, row)
+        edges.append((row[0], row[-1]))
+        if lon in (0, lons - 2):
+            kept[lon] = row
+        if lon == 1:
+            b_out.put(0, pair(kept[0], row)[1])
+        if lon == lons - 1:
+            a_out.put(0, pair(kept[lons - 2], row)[0])
     for within in range(groups):
         to_left = to_right = None
         for group in range(4):
-            lon = groups * group + within
             here = (k.l >> 5) == group
-            a = turn(x_refs[0][pl.ds(lon, block, stride=lons), :], HALO * group)
-            b = turn(x_refs[-1][pl.ds(lon, block, stride=lons), :], HALO * group - (LANES - HALO))
+            a, b = edges[groups * group + within]
+            a, b = turn(a, HALO * group), turn(b, HALO * group - (LANES - HALO))
             to_left = a if to_left is None else jnp.where(here, a, to_left)
             to_right = b if to_right is None else jnp.where(here, b, to_right)
-        to_left_ref[within] = to_left
-        to_right_ref[within, at, :] = to_right
+        to_left_out.put(within, [to_left])
+        to_right_out.put(within, [to_right])
 
     @pl.when(pl.program_id(0) == 0)
     def _():
@@ -247,9 +281,8 @@
 
 def weights_kernel(index_ref, table_ref, halo_ref, out_ref, arranged_ref):
     l = lax.broadcasted_iota(jnp.int32, (SUB, LANES), 1)
-    block = out_ref.shape[1]
-    table = get(table_ref, 0, table_ref.shape[1] // LANES)
-    halo = jnp.where(l >= LANES - 16, halo_ref[0], 0.0)
+    table = [table_ref[:, pl.ds(LANES * v, LANES)] for v in range(table_ref.shape[1] // LANES)]
+    halo = jnp.where(l >= LANES - 16, halo_ref[0, pl.ds(halo_ref.shape[1] - SUB, SUB), :], 0.0)
     for level in range(LEVELS):
         scale = tap_1 ** (4 * (level + 1))
         mains = MAINS[level]
@@ -272,11 +305,12 @@
             table_row = index_ref[3 * level + band]
             for i in range(mains + 1):
                 out_ref[WEIGHTS[level, band] + i] = jnp.broadcast_to(
-                    arranged_ref[i, pl.ds(table_row, 1), :], (block, LANES)
+                    arranged_ref[i, pl.ds(table_row, 1), :], (SUB, LANES)
                 )
 
 
-def send_kernel(lons, block, x_refs, left_ref, right_ref, c1_ref, to_right, to_left, far_right, far_left):
+def send_kernel(lons, block, *refs):
+    x_refs, left_ref, right_ref, c1_ref, to_right, to_left, far_right, far_left = views(block, refs)
     k = Lanes(block)
     many = Stacks(block)
     half = lons // 2
@@ -347,12 +381,13 @@
     put(to_left, LEFT["edge"], edges_left)
 
 
-def inner_kernel(lons, block, w_ref, x_refs, left_ref, right_ref, out_ref):
+def inner_kernel(lons, block, w_ref, *refs):
+    x_refs, left_ref, right_ref, out_ref = views(block, refs)
     k = Lanes(block)
     half = lons // 2
 
     def weight(band):
-        return [w_ref[WEIGHTS[0, band] + i] for i in range(5)]
+        return weight_of(w_ref, block, 0, band)
 
     def store(p, a, b):
         y0, y1 = unpair(a, b)
@@ -392,25 +427,10 @@
     store(half - 1, [k.zero] * len(before), before)
 
 
-def outer_kernel(
-    lons,
-    block,
-    w_ref,
-    part_ref,
-    c1_ref,
-    own_a,
-    own_b,
-    own_right,
-    own_left,
-    left_a,
-    right_b,
-    from_left,
-    from_right,
-    far_left,
-    far_right,
-    out_ref,
-    y_ref,
-):
+def outer_kernel(lons, block, w_ref, *refs):
+    part_ref, c1_ref, own_a, own_b, own_right, own_left = views(block, refs[:6])
+    left_a, right_b, from_left, from_right, far_left, far_right = views(block, refs[6:12])
+    out_ref, y_ref = refs[12:]
     many = Stacks(block)
     half = lons // 2
 
@@ -422,7 +442,7 @@
         return get(ref, places[name], COUNT[name]) + [edge(ref, name, places)]
 
     def weight(level, band):
-        return [w_ref[WEIGHTS[level, band] + i] for i in range(MAINS[level] + 1)]
+        return weight_of(w_ref, block, level, band)
 
     def inner(level, rows, a_first, b_last):
         pairs = [pair(rows[2 * i], rows[2 * i + 1]) for i in range(len(rows) // 2)]
@@ -447,7 +467,7 @@
             field.extend(unpair(a[i], b[i - 1]))
         return field
 
-    count = own_a.shape[1] // LANES
+    count = own_a.ref.shape[0]
     a_first = get(left_a, 0, count) + [edge(from_left, "a0", RIGHT)]
     b_first = get(own_b, 0, count) + [edge(own_left, "b0", LEFT)]
     a_last = get(own_a, 0, count) + [edge(own_right, "a0", RIGHT)]
@@ -512,38 +532,33 @@
 
 def per_device(perturbation, weight_table, band_index):
     members, lons, lats = perturbation.shape
-    assert lons == 16 and lats == 8 * LANES and members % BLOCK == 0
-    block = BLOCK
-    steps = members // block
+    assert lons == 16 and lats == 8 * LANES and members % SUB == 0
     x = perturbation.reshape(members * lons, lats)
-    shape = lambda *dims: jax.ShapeDtypeStruct(dims, jnp.float32)
+    registers = lambda count, rows=members: jax.ShapeDtypeStruct((count, rows, LANES), jnp.float32)
+    whole = pl.BlockSpec(memory_space=pltpu.VMEM)
     groups = lons // 4
     cols = lats // LANES
-    params = pltpu.CompilerParams(vmem_limit_bytes=60 * 1024 * 1024)
-    by_member = lambda width: pl.BlockSpec((block, width), lambda i: (i, 0))
-    x_specs = [pl.BlockSpec((block * lons, LANES), lambda i, v=v: (i, v)) for v in range(cols)]
-    halo_spec = pl.BlockSpec((groups, block, LANES), lambda i: (0, i, 0))
-    w_spec = pl.BlockSpec((WEIGHT_COUNT, block, LANES), lambda i: (0, 0, 0))
-
-    to_left, to_right, own_a, own_b = pl.pallas_call(
-        lambda *refs: first_kernel(lons, block, refs[:cols], *refs[cols:]),
-        grid=(steps,),
-        in_specs=x_specs + [pl.BlockSpec((SUB, LANES), lambda i: (0, lats // 2 // LANES - 1))],
-        out_specs=[
-            halo_spec,
-            pl.BlockSpec((groups, members + SUB, LANES), lambda i: (0, 0, 0)),
-            by_member(lats),
-            by_member(lats),
-        ],
-        out_shape=[
-            shape(groups, members, LANES),
-            shape(groups, members + SUB, LANES),
-            shape(members, lats),
-            shape(members, lats),
-        ],
-        compiler_params=params,
-        name="first",
-    )(*[x] * cols, weight_table)
+
+    def call(kernel, block, outs, megabytes, **more):
+        block = block if members % block == 0 else SUB
+        return pl.pallas_call(
+            lambda *refs: kernel(lons, block, *refs),
+            grid=(members // block,),
+            out_shape=outs,
+            compiler_params=pltpu.CompilerParams(vmem_limit_bytes=megabytes * 1024 * 1024),
+            **more,
+        )
+
+    block = FIRST_BLOCK if members % FIRST_BLOCK == 0 else SUB
+    xt, to_left, to_right, own_a, own_b = call(
+        lambda lons, block, *refs: first_kernel(lons, block, refs[:cols], *refs[cols:]),
+        FIRST_BLOCK,
+        [registers(lons * cols), registers(groups), registers(groups, members + SUB), registers(cols), registers(cols)],
+        24,
+        in_specs=[pl.BlockSpec((block * lons, LANES), lambda i, v=v: (i, v)) for v in range(cols)]
+        + [pl.BlockSpec((SUB, LANES), lambda i: (0, lats // 2 // LANES - 1))],
+        out_specs=[whole] * 5,
+    )(*[pltpu.with_memory_space_constraint(x, pltpu.HBM)] * cols, pltpu.with_memory_space_constraint(weight_table, pltpu.HBM))
     before = shift(to_right, "lat", 1, False)
     beyond = shift(to_left, "lat", -1, False)
     left_a = shift(own_a, "lon", 1, True)
@@ -551,65 +566,47 @@
 
     weights = pl.pallas_call(
         weights_kernel,
-        grid=(1,),
-        in_specs=[
-            pl.BlockSpec(memory_space=pltpu.SMEM),
-            pl.BlockSpec((SUB, lats // 2), lambda i: (0, 0)),
-            pl.BlockSpec((1, SUB, LANES), lambda i: (0, members // SUB, 0)),
-        ],
-        out_specs=pl.BlockSpec((WEIGHT_COUNT, block, LANES), lambda i: (0, 0, 0)),
-        out_shape=shape(WEIGHT_COUNT, block, LANES),
+        in_specs=[pl.BlockSpec(memory_space=pltpu.SMEM), whole, whole],
+        out_specs=whole,
+        out_shape=registers(WEIGHT_COUNT, SUB),
         scratch_shapes=[pltpu.VMEM((5, SUB, LANES), jnp.float32)],
-        compiler_params=params,
+        compiler_params=pltpu.CompilerParams(vmem_limit_bytes=8 * 1024 * 1024),
         name="weights",
     )(band_index, weight_table, before)
 
-    c1_width = (lons // 2 - 1) * 5 * LANES
-    right_width, left_width = RIGHT_SIZE * LANES, LEFT_SIZE * LANES
-    c1, to_right, to_left, far_right, far_left = pl.pallas_call(
-        lambda *refs: send_kernel(lons, block, refs[:cols], *refs[cols:]),
-        grid=(steps,),
-        in_specs=x_specs + [halo_spec, halo_spec],
-        out_specs=[by_member(c1_width), by_member(right_width), by_member(left_width)] + [by_member(2 * LANES)] * 2,
-        out_shape=[
-            shape(members, c1_width),
-            shape(members, right_width),
-            shape(members, left_width),
-            shape(members, 2 * LANES),
-            shape(members, 2 * LANES),
-        ],
-        compiler_params=params,
+    c1, to_right, to_left, far_right, far_left = call(
+        send_kernel,
+        SEND_BLOCK,
+        [registers(n) for n in ((lons // 2 - 1) * 5, RIGHT_SIZE, LEFT_SIZE, 2, 2)],
+        24,
+        in_specs=[whole] * 3,
+        out_specs=[whole] * 5,
         cost_estimate=pl.CostEstimate(flops=10**7, bytes_accessed=10**7, transcendentals=0),
-        name="send",
-    )(*[x] * cols, before, beyond)
+    )(xt, before, beyond)
     from_left = shift(to_right, "lon", 1, True)
     from_right = shift(to_left, "lon", -1, True)
     from_far_left = shift(far_right, "lon", 2, True)
     from_far_right = shift(far_left, "lon", -2, True)
 
-    part = pl.pallas_call(
-        lambda *refs: inner_kernel(lons, block, refs[0], refs[1 : cols + 1], *refs[cols + 1 :]),
-        grid=(steps,),
-        in_specs=[w_spec] + x_specs + [halo_spec, halo_spec],
-        out_specs=by_member(lons * lats),
-        out_shape=shape(members, lons * lats),
-        compiler_params=params,
+    part = call(
+        inner_kernel,
+        INNER_BLOCK,
+        registers(lons * cols),
+        24,
+        in_specs=[whole] * 4,
+        out_specs=whole,
         cost_estimate=pl.CostEstimate(flops=10**7, bytes_accessed=4 * 10**7, transcendentals=0),
-        name="inner",
-    )(weights, *[x] * cols, before, beyond)
-
-    out = pl.pallas_call(
-        lambda *refs: outer_kernel(lons, block, *refs),
-        grid=(steps,),
-        in_specs=[w_spec, by_member(lons * lats), by_member(c1_width), by_member(lats), by_member(lats)]
-        + [by_member(right_width), by_member(left_width), by_member(lats), by_member(lats)]
-        + [by_member(right_width), by_member(left_width)]
-        + [by_member(2 * LANES)] * 2,
+    )(weights, xt, before, beyond)
+
+    block = OUTER_BLOCK if members % OUTER_BLOCK == 0 else SUB
+    out = call(
+        outer_kernel,
+        OUTER_BLOCK,
+        jax.ShapeDtypeStruct((members * lons, lats), jnp.float32),
+        28,
+        in_specs=[whole] * 13,
         out_specs=pl.BlockSpec((block * lons, lats), lambda i: (i, 0)),
-        out_shape=shape(members * lons, lats),
         scratch_shapes=[pltpu.VMEM((cols, block * lons, LANES), jnp.float32)],
-        compiler_params=params,
-        name="outer",
     )(
         weights,
         part,

time: 75.2 us -> 64.2 us (0.85)
  Pallas kernels: 36.9 us -> 24 us
  waiting for transfers between devices: 20.5 us -> 25.3 us
  local copies, waits for them, and re-layouts: 2.49 us -> 0.01 us
    pallas_call x5, Pallas kernels: 36.9 us -> 24 us  [the longest x1 9.91 us: per_device(): call(outer_kernel, OUTER_BLOCK, jax.ShapeDtypeStruct((members * lons, lat...]
    ppermute x8, waiting for transfers between devices: 20.5 us -> 25.3 us  [shift(): return lax.ppermute(x, axis, pairs)]
    unnamed x20 -> x4, local copies, waits for them, and re-layouts: 2.49 us -> 0.01 us
  transfers between devices with their start and end apart: 8 -> 8, of which waited for: 2 -> 4; matrix products, arithmetic and copies ran while one was open for 0% -> 0% of each run, Pallas kernels for 16% -> 10%
where the time goes in v1:
time: 64.2 us; the launch traced here: 63.6 us
  waiting for transfers between devices  25.3 us (39%)
  Pallas kernels  24 us (37%)
  starting transfers between devices  14.3 us (22%)
    ppermute x8, waiting for transfers between devices, shift(): return lax.ppermute(x, axis, pairs)  25.3 us
    ppermute x8, starting transfers between devices, shift(): return lax.ppermute(x, axis, pairs)  14.3 us
    pallas_call x1, Pallas kernels, per_device(): call(outer_kernel, OUTER_BLOCK, jax.ShapeDtypeStruct((members * lons, lat...  9.91 us
    pallas_call x1, Pallas kernels, per_device(): call(inner_kernel, INNER_BLOCK, registers(lons * cols), 24, in_specs=[who...  5.77 us
    pallas_call x1, Pallas kernels, per_device(): call(lambda lons, block, *refs: first_kernel(lons, block, refs[:cols], *r...  4.08 us
    pallas_call x1, Pallas kernels, per_device(): call(send_kernel, SEND_BLOCK, [registers(n) for n in ((lons // 2 - 1) * 5...  3.51 us
  transfers between devices with their start and end apart: 8, of which 4 were waited for; matrix products, arithmetic and copies ran while one was open for 0% of the time, Pallas kernels for 10%

profile of v1, /device:TPU:1, one launch (start us, length us, event | category | flops | bytes accessed | tf_op | source)
XLA Modules:
  0.0 63.6 jit_solution(11819162928389518983)
XLA Ops:
  0.0 4.1 %shard_map.37 = (f32[128,80,128]{2,1,0:T(8,128)S(1)}, f32[4,80,128]{2,1,0:T(8,128)S(1)}, f32[4,88,128]{2,1,0:T(8,128)S(1)}, f32[8,80,128]{2,1,0:T(8,128)S(1)}, f32[8,80,128]{2,1,0:T(8,128)S(1)}) custom-call(f32[1280,1024]{1,0:T(8,128)} %bitcast.2, f32[1280,1024]{1,0:T(8,128)} %bitcast.3, f32[1280,1024]{1,0:T(8,128)} %bitcast.4, f32[1280,1024]{1,0:T(8,128)} %bitcast.5, ...), custom_call_target="tpu_custom_call" | custom-call | tf_op jit(solution)/shard_map/pallas_call | solution.py:553
  4.1 0.0 copy-start
  4.1 0.0 copy-start.1
  4.1 4.5 %collective-permute-start = (f32[4,88,128]{2,1,0:T(8,128)S(1)}, f32[4,88,128]{2,1,0:T(8,128)S(1)}, u32[]{:S(2)}, u32[]{:S(2)}) collective-permute-start(f32[4,88,128]{2,1,0:T(8,128)S(1)} %get-tuple-element.15), channel_id=1, source_target_pairs={{0,1},{1,2},{2,3},{4,5},{5,6},{6,7},{8,9},{9,10},{10,11},{12,13},{... | collective-permute-start | bytes 540680 | tf_op jit(solution)/shard_map/ppermute | solution.py:530
  8.6 1.9 %collective-permute-start.1 = (f32[4,80,128]{2,1,0:T(8,128)S(1)}, f32[4,80,128]{2,1,0:T(8,128)S(1)}, u32[]{:S(2)}, u32[]{:S(2)}) collective-permute-start(f32[4,80,128]{2,1,0:T(8,128)S(1)} %get-tuple-element.17), channel_id=1, source_target_pairs={{1,0},{2,1},{3,2},{5,4},{6,5},{7,6},{9,8},{10,9},{11,10},{13,12},{... | collective-permute-start | bytes 491528 | tf_op jit(solution)/shard_map/ppermute | solution.py:530
  10.5 4.7 %collective-permute-done.1.refs_3_.refs_2_ = f32[4,80,128]{2,1,0:T(8,128)S(1)} collective-permute-done((f32[4,80,128]{2,1,0:T(8,128)S(1)}, f32[4,80,128]{2,1,0:T(8,128)S(1)}, u32[]{:S(2)}, u32[]{:S(2)}) %collective-permute-start.1) | collective-permute-done | bytes 163872 | tf_op jit(solution)/shard_map/ppermute | solution.py:530
  15.3 0.0 collective-permute-done.halo_ref.refs_2_.refs_1_
  15.3 3.5 %shard_map.39 = (f32[35,80,128]{2,1,0:T(8,128)S(1)}, f32[13,80,128]{2,1,0:T(8,128)S(1)}, f32[8,80,128]{2,1,0:T(8,128)S(1)}, f32[2,80,128]{2,1,0:T(8,128)S(1)}, f32[2,80,128]{2,1,0:T(8,128)S(1)}) custom-call(f32[128,80,128]{2,1,0:T(8,128)S(1)} %get-tuple-element.16.refs_1_.refs_0_, f32[4,88,128]{2,1,0:T(8,128)S(1)} %collective-permute-done.halo_ref.refs_2_.refs_1_, ...), custom_call_target="tpu_custom_call" | custom-call | flops 10000000 | bytes 10000000 | tf_op jit(solution)/shard_map/pallas_call | solution.py:577
  18.8 1.3 %collective-permute-start.4 = (f32[13,80,128]{2,1,0:T(8,128)S(1)}, f32[13,80,128]{2,1,0:T(8,128)S(1)}, u32[]{:S(2)}, u32[]{:S(2)}) collective-permute-start(f32[13,80,128]{2,1,0:T(8,128)S(1)} %get-tuple-element.21.refs_5_), channel_id=1, source_target_pairs={{0,4},{4,8},{8,12},{12,16},{16,20},{20,24},{24,28},{28,0},{1,5},{5... | collective-permute-start | bytes 1597448 | tf_op jit(solution)/shard_map/ppermute | solution.py:530
  20.1 1.2 %collective-permute-start.2 = (f32[8,80,128]{2,1,0:T(8,128)S(1)}, f32[8,80,128]{2,1,0:T(8,128)S(1)}, u32[]{:S(2)}, u32[]{:S(2)}) collective-permute-start(f32[8,80,128]{2,1,0:T(8,128)S(1)} %get-tuple-element.19.refs_3_), channel_id=1, source_target_pairs={{0,4},{4,8},{8,12},{12,16},{16,20},{20,24},{24,28},{28,0},{1,5},{5... | collective-permute-start | bytes 983048 | tf_op jit(solution)/shard_map/ppermute | solution.py:530
  21.3 2.9 %collective-permute-start.3 = (f32[8,80,128]{2,1,0:T(8,128)S(1)}, f32[8,80,128]{2,1,0:T(8,128)S(1)}, u32[]{:S(2)}, u32[]{:S(2)}) collective-permute-start(f32[8,80,128]{2,1,0:T(8,128)S(1)} %get-tuple-element.20.refs_4_), channel_id=1, source_target_pairs={{0,28},{4,0},{8,4},{12,8},{16,12},{20,16},{24,20},{28,24},{1,29},{... | collective-permute-start | bytes 983048 | tf_op jit(solution)/shard_map/ppermute | solution.py:530
  24.2 0.4 collective-permute-start.5
  24.6 0.0 collective-permute-start.6
  24.6 15.6 %collective-permute-done.6.refs_11_ = f32[2,80,128]{2,1,0:T(8,128)S(1)} collective-permute-done((f32[2,80,128]{2,1,0:T(8,128)S(1)}, f32[2,80,128]{2,1,0:T(8,128)S(1)}, u32[]{:S(2)}, u32[]{:S(2)}) %collective-permute-start.6) | collective-permute-done | bytes 81952 | tf_op jit(solution)/shard_map/ppermute | solution.py:530
  40.2 2.0 %collective-permute-start.7 = (f32[2,80,128]{2,1,0:T(8,128)S(1)}, f32[2,80,128]{2,1,0:T(8,128)S(1)}, u32[]{:S(2)}, u32[]{:S(2)}) collective-permute-start(f32[2,80,128]{2,1,0:T(8,128)S(1)} %get-tuple-element.24), channel_id=1, source_target_pairs={{0,24},{4,28},{8,0},{12,4},{16,8},{20,12},{24,16},{28,20},{1,25},{... | collective-permute-start | bytes 245768 | tf_op jit(solution)/shard_map/ppermute | solution.py:530
  42.2 0.0 copy-done
  42.2 0.0 copy-done.1
  42.2 0.7 %weights.1.refs_0_ = f32[38,8,128]{2,1,0:T(8,128)S(1)} custom-call(s32[13]{0:T(128)S(1)} %copy-done.1, f32[8,512]{1,0:T(8,128)S(1)} %copy-done, f32[4,88,128]{2,1,0:T(8,128)S(1)} %collective-permute-done.halo_ref.refs_2_.refs_1_), custom_call_target="tpu_custom_call" | custom-call | tf_op jit(solution)/shard_map/weights/pallas_call | solution.py:567
  42.9 5.8 %shard_map.38.refs_1_ = f32[128,80,128]{2,1,0:T(8,128)S(1)} custom-call(f32[38,8,128]{2,1,0:T(8,128)S(1)} %weights.1.refs_0_, f32[128,80,128]{2,1,0:T(8,128)S(1)} %get-tuple-element.16.refs_1_.refs_0_, f32[4,88,128]{2,1,0:T(8,128)S(1)} %collective-permute-done.halo_ref.refs_2_.refs_1_, f32[4,80,128]{2,1,0:T(8,128)S(1)} %collective-permute-done.1.refs_3_.refs_2_), custom_call_target="tpu_custom_call" | custom-call | flops 10000000 | bytes 40000000 | tf_op jit(solution)/shard_map/pallas_call | solution.py:591
  48.7 0.0 collective-permute-done.7.refs_12_
  48.7 1.5 %collective-permute-done.2.refs_7_ = f32[8,80,128]{2,1,0:T(8,128)S(1)} collective-permute-done((f32[8,80,128]{2,1,0:T(8,128)S(1)}, f32[8,80,128]{2,1,0:T(8,128)S(1)}, u32[]{:S(2)}, u32[]{:S(2)}) %collective-permute-start.2) | collective-permute-done | bytes 327712 | tf_op jit(solution)/shard_map/ppermute | solution.py:530
  50.2 0.0 collective-permute-done.3.refs_8_
  50.2 3.6 %collective-permute-done.5.refs_10_ = f32[8,80,128]{2,1,0:T(8,128)S(1)} collective-permute-done((f32[8,80,128]{2,1,0:T(8,128)S(1)}, f32[8,80,128]{2,1,0:T(8,128)S(1)}, u32[]{:S(2)}, u32[]{:S(2)}) %collective-permute-start.5) | collective-permute-done | bytes 327712 | tf_op jit(solution)/shard_map/ppermute | solution.py:530
  53.7 0.0 collective-permute-done.4.refs_9_
  53.7 9.9 %shard_map.40 = f32[1280,1024]{1,0:T(8,128)} custom-call(f32[38,8,128]{2,1,0:T(8,128)S(1)} %weights.1.refs_0_, f32[128,80,128]{2,1,0:T(8,128)S(1)} %shard_map.38.refs_1_, f32[35,80,128]{2,1,0:T(8,128)S(1)} %get-tuple-element.18.refs_2_, f32[8,80,128]{2,1,0:T(8,128)S(1)} %get-tuple-element.19.refs_3_, f32[8,80,128]{2,1,0:T(8,128)S(1)} %get-tuple-element.20.refs_4_, ...), custom_call_target="tpu_custom_call" | custom-call | tf_op jit(solution)/shard_map/pallas_call | solution.py:602
Async XLA Ops:
  4.1 38.1 %copy-start = (f32[8,512]{1,0:T(8,128)S(1)}, f32[8,512]{1,0:T(8,128)}, u32[]{:S(2)}) copy-start(f32[8,512]{1,0:T(8,128)} %table_ref.1) | copy-start | bytes 49156
  4.1 38.1 %copy-start.1 = (s32[13]{0:T(128)S(1)}, s32[13]{0:T(128)}, u32[]{:S(2)}) copy-start(s32[13]{0:T(128)} %index_ref.1) | copy-start | bytes 160
  4.1 11.1 %collective-permute-start = (f32[4,88,128]{2,1,0:T(8,128)S(1)}, f32[4,88,128]{2,1,0:T(8,128)S(1)}, u32[]{:S(2)}, u32[]{:S(2)}) collective-permute-start(f32[4,88,128]{2,1,0:T(8,128)S(1)} %get-tuple-element.15), channel_id=1, source_target_pairs={{0,1},{1,2},{2,3},{4,5},{5,6},{6,7},{8,9},{9,10},{10,11},{12,13},{... | collective-permute-start | bytes 540680 | tf_op jit(solution)/shard_map/ppermute | solution.py:530
  8.6 6.6 %collective-permute-start.1 = (f32[4,80,128]{2,1,0:T(8,128)S(1)}, f32[4,80,128]{2,1,0:T(8,128)S(1)}, u32[]{:S(2)}, u32[]{:S(2)}) collective-permute-start(f32[4,80,128]{2,1,0:T(8,128)S(1)} %get-tuple-element.17), channel_id=1, source_target_pairs={{1,0},{2,1},{3,2},{5,4},{6,5},{7,6},{9,8},{10,9},{11,10},{13,12},{... | collective-permute-start | bytes 491528 | tf_op jit(solution)/shard_map/ppermute | solution.py:530
  18.8 35.0 %collective-permute-start.4 = (f32[13,80,128]{2,1,0:T(8,128)S(1)}, f32[13,80,128]{2,1,0:T(8,128)S(1)}, u32[]{:S(2)}, u32[]{:S(2)}) collective-permute-start(f32[13,80,128]{2,1,0:T(8,128)S(1)} %get-tuple-element.21.refs_5_), channel_id=1, source_target_pairs={{0,4},{4,8},{8,12},{12,16},{16,20},{20,24},{24,28},{28,0},{1,5},{5... | collective-permute-start | bytes 1597448 | tf_op jit(solution)/shard_map/ppermute | solution.py:530
  20.1 30.1 %collective-permute-start.2 = (f32[8,80,128]{2,1,0:T(8,128)S(1)}, f32[8,80,128]{2,1,0:T(8,128)S(1)}, u32[]{:S(2)}, u32[]{:S(2)}) collective-permute-start(f32[8,80,128]{2,1,0:T(8,128)S(1)} %get-tuple-element.19.refs_3_), channel_id=1, source_target_pairs={{0,4},{4,8},{8,12},{12,16},{16,20},{20,24},{24,28},{28,0},{1,5},{5... | collective-permute-start | bytes 983048 | tf_op jit(solution)/shard_map/ppermute | solution.py:530
  21.3 28.9 %collective-permute-start.3 = (f32[8,80,128]{2,1,0:T(8,128)S(1)}, f32[8,80,128]{2,1,0:T(8,128)S(1)}, u32[]{:S(2)}, u32[]{:S(2)}) collective-permute-start(f32[8,80,128]{2,1,0:T(8,128)S(1)} %get-tuple-element.20.refs_4_), channel_id=1, source_target_pairs={{0,28},{4,0},{8,4},{12,8},{16,12},{20,16},{24,20},{28,24},{1,29},{... | collective-permute-start | bytes 983048 | tf_op jit(solution)/shard_map/ppermute | solution.py:530
  24.2 29.5 %collective-permute-start.5 = (f32[8,80,128]{2,1,0:T(8,128)S(1)}, f32[8,80,128]{2,1,0:T(8,128)S(1)}, u32[]{:S(2)}, u32[]{:S(2)}) collective-permute-start(f32[8,80,128]{2,1,0:T(8,128)S(1)} %get-tuple-element.22.refs_6_), channel_id=1, source_target_pairs={{0,28},{4,0},{8,4},{12,8},{16,12},{20,16},{24,20},{28,24},{1,29},{... | collective-permute-start | bytes 983048 | tf_op jit(solution)/shard_map/ppermute | solution.py:530
  24.6 15.6 %collective-permute-start.6 = (f32[2,80,128]{2,1,0:T(8,128)S(1)}, f32[2,80,128]{2,1,0:T(8,128)S(1)}, u32[]{:S(2)}, u32[]{:S(2)}) collective-permute-start(f32[2,80,128]{2,1,0:T(8,128)S(1)} %get-tuple-element.23), channel_id=1, source_target_pairs={{0,8},{4,12},{8,16},{12,20},{16,24},{20,28},{24,0},{28,4},{1,9},{5... | collective-permute-start | bytes 245768 | tf_op jit(solution)/shard_map/ppermute | solution.py:530
  40.2 8.5 %collective-permute-start.7 = (f32[2,80,128]{2,1,0:T(8,128)S(1)}, f32[2,80,128]{2,1,0:T(8,128)S(1)}, u32[]{:S(2)}, u32[]{:S(2)}) collective-permute-start(f32[2,80,128]{2,1,0:T(8,128)S(1)} %get-tuple-element.24), channel_id=1, source_target_pairs={{0,24},{4,28},{8,0},{12,4},{16,8},{20,12},{24,16},{28,20},{1,25},{... | collective-permute-start | bytes 245768 | tf_op jit(solution)/shard_map/ppermute | solution.py:530
